TPU v7x, 32 devices: a whole 2x2x4 slice. The times are simulated.
32 devices in a mesh: fsdp: 8 (over y, x, core), ep: 4 (over z).
Axes of the slice: x: 2, y: 2, z: 4, core: 2. Of those that a mesh axis runs over, the one named last changes fastest.
Arguments:
- hidden: bfloat16 [2048, 8192], P('fsdp', 'ep'), may hold values from -6 to 6
- w_down: bfloat16 [6144, 2, 8192], P('fsdp', None, 'ep'), may hold values from -0.0625 to 0.0625
- route_ids: int32 [1024, 2], P('fsdp'), may hold values from 0 to 7, as said below
- probs: float32 [1024, 2], P('fsdp'), may hold values from 0.1 to 0.9
- grad_out: bfloat16 [1024, 6144], P('fsdp', 'ep'), may hold values from -6 to 6
Outputs:
- output: bfloat16 [1024, 6144], P('fsdp', 'ep')
- grad_hidden: bfloat16 [2048, 8192], P('fsdp', 'ep')
- grad_weight: bfloat16 [6144, 2, 8192], P('fsdp', None, 'ep')
- grad_probs: float32 [1024, 2], P('fsdp')
Inputs may be any that keep to these rules, and one draw needn't show every extreme that they name: `route_ids`: each token names 2 different experts. Within one panel's 128 tokens, experts 0 and 1 are each named by 1 to 128 tokens, and in some panel both are named by all 128 tokens.
All inputs are finite; a program needn't handle non-finite values.
Results may differ from a plain program's by a relative error of at most 0.012.
Values may be sent and summed in bfloat16 or wider, within the bound.
A program may use at most 384 MiB of HBM per device.

v0:
```python
import jax
import jax.numpy as jnp
from jax import lax
from jax.sharding import PartitionSpec as P

BLOCK = 128


def route_layout(route_part, prob_part, expert_count, block_rows, row_count):
    token_count = route_part.shape[0]
    experts = jnp.arange(expert_count, dtype=jnp.int32)
    hits = (route_part[:, :, None] == experts[None, None, :]).astype(jnp.int32)
    named = jnp.sum(hits, axis=1)
    counts = jnp.sum(named, axis=0)
    ranks = jnp.cumsum(named, axis=0) - named
    padded = (counts + block_rows - 1) // block_rows * block_rows
    offsets = jnp.cumsum(padded) - padded
    row_of = jnp.sum(hits * (offsets[None, None, :] + ranks[:, None, :]), axis=2)
    valid = jnp.sum(hits, axis=2)
    starts = jnp.arange(row_count // block_rows, dtype=jnp.int32) * block_rows
    inside = (starts[:, None] >= offsets[None, :]) & (starts[:, None] < (offsets + padded)[None, :])
    block_exp = jnp.sum(jnp.where(inside, experts[None, :] + 1, 0), axis=1) - 1
    target = jnp.where(valid > 0, row_of, row_count).reshape(-1)
    token_index = jnp.broadcast_to(
        jnp.arange(token_count, dtype=jnp.int32)[:, None], route_part.shape
    ).reshape(-1)
    row_tok = jnp.zeros((row_count,), jnp.int32).at[target].set(token_index, mode="drop")
    row_live = (
        jnp.zeros((row_count,), jnp.int32).at[target].set(jnp.ones_like(token_index), mode="drop")
    )
    row_prob = (
        jnp.zeros((row_count,), prob_part.dtype).at[target].set(prob_part.reshape(-1), mode="drop")
    )
    return (row_of, valid, block_exp, row_tok, row_live, row_prob)


def local(hidden, w_down, route_ids, probs, grad_out):
    row_count, unit_count = hidden.shape
    expert_count = w_down.shape[1]
    block_count = row_count // BLOCK
    row_of, valid, block_exp, row_tok, row_live, row_prob = route_layout(
        route_ids, probs, expert_count, BLOCK, row_count
    )
    safe_exp = jnp.maximum(block_exp, 0)
    prob_valid = probs * valid.astype(jnp.float32)
    full_grads = lax.all_gather(grad_out, "ep", axis=1, tiled=True)
    model_width = full_grads.shape[1]
    routed = jnp.where(row_live[:, None] > 0, full_grads[row_tok], jnp.zeros((), jnp.bfloat16))
    scaled = (row_prob[:, None] * routed.astype(jnp.float32)).astype(jnp.bfloat16)
    hid_blocks = hidden.reshape(block_count, BLOCK, unit_count)
    routed_blocks = routed.reshape(block_count, BLOCK, model_width)
    row_exp = jnp.repeat(block_exp, BLOCK)
    member = (row_exp[:, None] == jnp.arange(expert_count, dtype=jnp.int32)[None, :]).astype(
        jnp.bfloat16
    )
    masked_hid = hidden[:, None, :] * member[:, :, None]
    piece = lax.all_gather(w_down, "fsdp", axis=0, tiled=True)
    width = piece.shape[0]
    chosen = jnp.take(piece, safe_exp, axis=1)
    out_rows = jnp.einsum(
        "bri,dbi->brd", hid_blocks, chosen, preferred_element_type=jnp.float32
    ).reshape(row_count, width)
    back_total = jnp.einsum(
        "brd,dbi->bri", routed_blocks, chosen, preferred_element_type=jnp.float32
    )
    combined = jnp.sum(prob_valid[:, :, None] * out_rows[row_of], axis=1)
    out_total = combined
    out_total, back_total = (out_total, back_total)
    grad_weight = lax.psum_scatter(
        jnp.einsum("rd,rei->dei", scaled, masked_hid, preferred_element_type=jnp.float32).astype(
            jnp.bfloat16
        ),
        "fsdp",
        scatter_dimension=0,
        tiled=True,
    )
    output = lax.psum_scatter(out_total.astype(jnp.bfloat16), "ep", scatter_dimension=1, tiled=True)
    hidden_back = back_total.reshape(row_count, unit_count)
    grad_hidden = (row_prob[:, None] * hidden_back).astype(jnp.bfloat16)
    row_dot = jnp.sum(hidden.astype(jnp.float32) * hidden_back, axis=1)
    prob_terms = valid.astype(jnp.float32) * row_dot[row_of]
    grad_probs = lax.psum(prob_terms, "ep")
    return (output, grad_hidden, grad_weight, grad_probs)


def solution(mesh):
    placed = (
        P("fsdp", "ep"),
        P("fsdp", None, "ep"),
        P("fsdp", None),
        P("fsdp", None),
        P("fsdp", "ep"),
    )
    return jax.shard_map(
        local,
        mesh=mesh,
        in_specs=placed,
        out_specs=(P("fsdp", "ep"), P("fsdp", "ep"), P("fsdp", None, "ep"), P("fsdp", None)),
        check_vma=False,
    )
```

profile of v0, /device:TPU:0, one launch (start us, length us, event | category | flops | bytes accessed | tf_op | source)
XLA Modules:
  0.0 635.5 jit_solution(14992355778642910269)
XLA Ops:
  7.9 8.4 %copy.21 = bf16[768,2,2048]{2,0,1:T(8,128)(2,1)} copy(bf16[768,2,2048]{2,1,0:T(2,128)(2,1)} %param.6) | data formatting | bytes 12582912 | tf_op args[1]
  23.5 25.9 %all-gather.5.cloned.1.call-done = bf16[128,6144]{1,0:T(8,128)(2,1)} async-done(((bf16[128,1536]{1,0:T(8,128)(2,1)}), bf16[128,6144]{1,0:T(8,128)(2,1)}) %all-gather.5.cloned.1.call-update) | async-done | bytes 1572880 | tf_op jit(solution)/shard_map/all_gather | solution.py:46
  49.4 7.1 %gather_fusion.1 = bf16[256,6144]{1,0:T(8,128)(2,1)S(1)} fusion(bf16[128,6144]{1,0:T(8,128)(2,1)} %all-gather.5.cloned.1.call-done, s32[1024]{0:T(1024)S(1)} %pad_clamp_fusion), kind=kCustom, calls=%fused_computation.1 | custom fusion | bytes 6292480 | tf_op jit(solution)/shard_map/gather | solution.py:48
  56.5 24.9 %convolution_convert_fusion = bf16[6144,2,2048]{2,0,1:T(8,128)(2,1)} fusion(bf16[256,6144]{1,0:T(8,128)(2,1)S(1)} %gather_fusion.1, f32[256]{0:T(256)S(1)} %scatter_custom_fusion, pred[256]{0:T(512)(128)(4,1)S(1)} %broadcast_compare_fusion, bf16[256,2]{0,1:T(2,128)(2,1)S(1)} %compare_convert_fusion, bf16[256,2048]{1,0:T(8,128)(2,1)} %param.5), kind=kOutput, calls=%fused_computation.31 | convolution fusion | flops 12920553472 | bytes 54528256 | tf_op jit(solution)/shard_map/rd,rei->dei/dot_general | solution.py:70
  83.2 199.5 %all-gather.3.cloned.1.call-done = bf16[6144,2,2048]{2,0,1:T(8,128)(2,1)} async-done(((bf16[768,2,2048]{2,0,1:T(8,128)(2,1)}), bf16[6144,2,2048]{2,0,1:T(8,128)(2,1)}) %all-gather.3.cloned.1.call-update) | async-done | bytes 50331664 | tf_op jit(solution)/shard_map/all_gather | solution.py:57
  282.7 41.5 %fusion.28 = (bf16[512,2,2048]{2,0,1:T(8,128)(2,1)}, bf16[512,2,2048]{2,0,1:T(8,128)(2,1)}, bf16[512,2,2048]{2,0,1:T(8,128)(2,1)}, bf16[512,2,2048]{2,0,1:T(8,12...) fusion(bf16[6144,2,2048]{2,0,1:T(8,128)(2,1)} %all-gather.3.clo, ...), kind=kLoop, calls=%fused_computation.108 | loop fusion | bytes 100663296 | tf_op jit(solution)/shard_map/jit(_take)/gather | solution.py:59
  324.2 3.0 broadcast.318.clone
  327.2 9.6 %while.12 = (s32[]{:T(128)}, bf16[512,2,2048]{2,0,1:T(8,128)(2,1)}, s32[2,1]{0,1:T(1,128)S(1)}, bf16[2,512,2048]{2,1,0:T(8,128)(2,1)}, s32[]{:T(128)}) while((s32[]{:T(128)}, bf16[512,2,2048]{2,0,1:T(8,128)(2,1)}, s32[2,1]{0,1:T(1,128)S(1)}, bf16[2,512,2048]{2,1,0:T(8,128)(2,1)}, s32[]{:T(128)}) %tuple.161), condition=%wide.while_cond, body=%wide.while_body.sunk | while | flops 2 | bytes 4195401 | solution.py:59
  327.8 4.2 bitcast_dynamic-update-slice_fusion.36
  332.5 4.3 bitcast_dynamic-update-slice_fusion.36
  336.8 3.1 broadcast.318.clone.1
  339.9 9.5 %while.13 = (s32[]{:T(128)}, bf16[512,2,2048]{2,0,1:T(8,128)(2,1)}, s32[2,1]{0,1:T(1,128)S(1)}, bf16[2,512,2048]{2,1,0:T(8,128)(2,1)}, s32[]{:T(128)}) while((s32[]{:T(128)}, bf16[512,2,2048]{2,0,1:T(8,128)(2,1)}, s32[2,1]{0,1:T(1,128)S(1)}, bf16[2,512,2048]{2,1,0:T(8,128)(2,1)}, s32[]{:T(128)}) %tuple.205), condition=%wide.while_cond.1, body=%wide.while_body.1.sunk | while | flops 2 | bytes 4195401 | solution.py:59
  340.5 4.3 bitcast_dynamic-update-slice_fusion.37
  345.4 4.0 bitcast_dynamic-update-slice_fusion.37
  349.4 2.6 broadcast.318.clone.2
  352.0 8.8 %while.14 = (s32[]{:T(128)}, bf16[512,2,2048]{2,0,1:T(8,128)(2,1)}, s32[2,1]{0,1:T(1,128)S(1)}, bf16[2,512,2048]{2,1,0:T(8,128)(2,1)}, s32[]{:T(128)}) while((s32[]{:T(128)}, bf16[512,2,2048]{2,0,1:T(8,128)(2,1)}, s32[2,1]{0,1:T(1,128)S(1)}, bf16[2,512,2048]{2,1,0:T(8,128)(2,1)}, s32[]{:T(128)}) %tuple.206), condition=%wide.while_cond.2, body=%wide.while_body.2.sunk | while | flops 2 | bytes 4195401 | solution.py:59
  352.5 3.8 bitcast_dynamic-update-slice_fusion.38
  356.9 3.9 bitcast_dynamic-update-slice_fusion.38
  360.8 2.6 broadcast.318.clone.3
  363.4 9.2 %while.15 = (s32[]{:T(128)}, bf16[512,2,2048]{2,0,1:T(8,128)(2,1)}, s32[2,1]{0,1:T(1,128)S(1)}, bf16[2,512,2048]{2,1,0:T(8,128)(2,1)}, s32[]{:T(128)}) while((s32[]{:T(128)}, bf16[512,2,2048]{2,0,1:T(8,128)(2,1)}, s32[2,1]{0,1:T(1,128)S(1)}, bf16[2,512,2048]{2,1,0:T(8,128)(2,1)}, s32[]{:T(128)}) %tuple.207), condition=%wide.while_cond.3, body=%wide.while_body.3.sunk | while | flops 2 | bytes 4195401 | solution.py:59
  363.9 4.1 bitcast_dynamic-update-slice_fusion.39
  368.6 3.9 bitcast_dynamic-update-slice_fusion.39
  372.6 2.6 broadcast.318.clone.4
  375.1 9.1 %while.16 = (s32[]{:T(128)}, bf16[512,2,2048]{2,0,1:T(8,128)(2,1)}, s32[2,1]{0,1:T(1,128)S(1)}, bf16[2,512,2048]{2,1,0:T(8,128)(2,1)}, s32[]{:T(128)}) while((s32[]{:T(128)}, bf16[512,2,2048]{2,0,1:T(8,128)(2,1)}, s32[2,1]{0,1:T(1,128)S(1)}, bf16[2,512,2048]{2,1,0:T(8,128)(2,1)}, s32[]{:T(128)}) %tuple.208), condition=%wide.while_cond.4, body=%wide.while_body.4.sunk | while | flops 2 | bytes 4195401 | solution.py:59
  375.7 3.9 bitcast_dynamic-update-slice_fusion.40
  380.1 4.1 bitcast_dynamic-update-slice_fusion.40
  384.2 2.5 broadcast.318.clone.5
  386.7 8.8 %while.17 = (s32[]{:T(128)}, bf16[512,2,2048]{2,0,1:T(8,128)(2,1)}, s32[2,1]{0,1:T(1,128)S(1)}, bf16[2,512,2048]{2,1,0:T(8,128)(2,1)}, s32[]{:T(128)}) while((s32[]{:T(128)}, bf16[512,2,2048]{2,0,1:T(8,128)(2,1)}, s32[2,1]{0,1:T(1,128)S(1)}, bf16[2,512,2048]{2,1,0:T(8,128)(2,1)}, s32[]{:T(128)}) %tuple.209), condition=%wide.while_cond.5, body=%wide.while_body.5.sunk | while | flops 2 | bytes 4195401 | solution.py:59
  387.3 3.8 bitcast_dynamic-update-slice_fusion.41
  391.6 3.8 bitcast_dynamic-update-slice_fusion.41
  395.5 2.6 broadcast.318.clone.6
  398.1 8.8 %while.18 = (s32[]{:T(128)}, bf16[512,2,2048]{2,0,1:T(8,128)(2,1)}, s32[2,1]{0,1:T(1,128)S(1)}, bf16[2,512,2048]{2,1,0:T(8,128)(2,1)}, s32[]{:T(128)}) while((s32[]{:T(128)}, bf16[512,2,2048]{2,0,1:T(8,128)(2,1)}, s32[2,1]{0,1:T(1,128)S(1)}, bf16[2,512,2048]{2,1,0:T(8,128)(2,1)}, s32[]{:T(128)}) %tuple.210), condition=%wide.while_cond.6, body=%wide.while_body.6.sunk | while | flops 2 | bytes 4195401 | solution.py:59
  398.6 3.8 bitcast_dynamic-update-slice_fusion.42
  403.0 3.9 bitcast_dynamic-update-slice_fusion.42
  406.9 2.5 broadcast.318.clone.7
  409.4 9.3 %while.19 = (s32[]{:T(128)}, bf16[512,2,2048]{2,0,1:T(8,128)(2,1)}, s32[2,1]{0,1:T(1,128)S(1)}, bf16[2,512,2048]{2,1,0:T(8,128)(2,1)}, s32[]{:T(128)}) while((s32[]{:T(128)}, bf16[512,2,2048]{2,0,1:T(8,128)(2,1)}, s32[2,1]{0,1:T(1,128)S(1)}, bf16[2,512,2048]{2,1,0:T(8,128)(2,1)}, s32[]{:T(128)}) %tuple.211), condition=%wide.while_cond.7, body=%wide.while_body.7.sunk | while | flops 2 | bytes 4195401 | solution.py:59
  410.0 4.2 bitcast_dynamic-update-slice_fusion.43
  414.8 4.0 bitcast_dynamic-update-slice_fusion.43
  421.2 8.8 %while.20 = (s32[]{:T(128)}, bf16[512,2,2048]{2,0,1:T(8,128)(2,1)}, s32[2,1]{0,1:T(1,128)S(1)}, bf16[2,512,2048]{2,1,0:T(8,128)(2,1)}, s32[]{:T(128)}) while((s32[]{:T(128)}, bf16[512,2,2048]{2,0,1:T(8,128)(2,1)}, s32[2,1]{0,1:T(1,128)S(1)}, bf16[2,512,2048]{2,1,0:T(8,128)(2,1)}, s32[]{:T(128)}) %tuple.212), condition=%wide.while_cond.8, body=%wide.while_body.8.sunk | while | flops 2 | bytes 4195401 | solution.py:59
  421.8 3.8 bitcast_dynamic-update-slice_fusion.44
  426.2 3.9 bitcast_dynamic-update-slice_fusion.44
  432.5 8.7 %while.21 = (s32[]{:T(128)}, bf16[512,2,2048]{2,0,1:T(8,128)(2,1)}, s32[2,1]{0,1:T(1,128)S(1)}, bf16[2,512,2048]{2,1,0:T(8,128)(2,1)}, s32[]{:T(128)}) while((s32[]{:T(128)}, bf16[512,2,2048]{2,0,1:T(8,128)(2,1)}, s32[2,1]{0,1:T(1,128)S(1)}, bf16[2,512,2048]{2,1,0:T(8,128)(2,1)}, s32[]{:T(128)}) %tuple.213), condition=%wide.while_cond.9, body=%wide.while_body.9.sunk | while | flops 2 | bytes 4195401 | solution.py:59
  433.1 3.8 bitcast_dynamic-update-slice_fusion.45
  437.5 3.8 bitcast_dynamic-update-slice_fusion.45
  441.3 2.6 broadcast.318.clone.10
  443.9 8.9 %while.22 = (s32[]{:T(128)}, bf16[512,2,2048]{2,0,1:T(8,128)(2,1)}, s32[2,1]{0,1:T(1,128)S(1)}, bf16[2,512,2048]{2,1,0:T(8,128)(2,1)}, s32[]{:T(128)}) while((s32[]{:T(128)}, bf16[512,2,2048]{2,0,1:T(8,128)(2,1)}, s32[2,1]{0,1:T(1,128)S(1)}, bf16[2,512,2048]{2,1,0:T(8,128)(2,1)}, s32[]{:T(128)}) %tuple.214), condition=%wide.while_cond.10, body=%wide.while_body.10.sunk | while | flops 2 | bytes 4195401 | solution.py:59
  444.5 3.9 bitcast_dynamic-update-slice_fusion.46
  448.9 3.9 bitcast_dynamic-update-slice_fusion.46
  452.8 2.5 broadcast.318.clone.11
  455.3 9.4 %while.23 = (s32[]{:T(128)}, bf16[512,2,2048]{2,0,1:T(8,128)(2,1)}, s32[2,1]{0,1:T(1,128)S(1)}, bf16[2,512,2048]{2,1,0:T(8,128)(2,1)}, s32[]{:T(128)}) while((s32[]{:T(128)}, bf16[512,2,2048]{2,0,1:T(8,128)(2,1)}, s32[2,1]{0,1:T(1,128)S(1)}, bf16[2,512,2048]{2,1,0:T(8,128)(2,1)}, s32[]{:T(128)}) %tuple.215), condition=%wide.while_cond.11, body=%wide.while_body.11.sunk | while | flops 2 | bytes 4195401 | solution.py:59
  455.9 4.1 bitcast_dynamic-update-slice_fusion.47
  460.6 4.2 bitcast_dynamic-update-slice_fusion.47
  464.7 5.3 bitcast_dynamic-update-slice_fusion.23
  477.7 2.5 bitcast_dynamic-update-slice_fusion.20
  500.2 2.5 bitcast_dynamic-update-slice_fusion.14
  510.1 25.9 %fusion.1 = f32[2,6144,128]{1,2,0:T(8,128)} fusion(bf16[2,128,2048]{2,1,0:T(8,128)(2,1)S(1)} %bitcast.149, bf16[6144,2,2048]{2,0,1:T(8,128)(2,1)} %bitcast_dynamic-update-slice_fusion.12, pred[2]{0:T(512)(128)(4,1)S(1)} %maximum_compare_fusion), kind=kOutput, calls=%fused_computation.33 | convolution fusion | flops 6467616768 | bytes 57671680 | tf_op jit(solution)/shard_map/bri,dbi->brd/dot_general | solution.py:60
  536.0 10.6 %gather_fusion = f32[256,6144]{1,0:T(8,128)} fusion(f32[256,6144]{1,0:T(8,128)} %bitcast.147, s32[1024]{0:T(1024)S(1)} %copy-done.14), kind=kCustom, calls=%fused_computation | custom fusion | bytes 12583936 | tf_op jit(solution)/shard_map/gather | solution.py:66
  546.6 8.4 %reshape.505 = f32[128,2,6144]{2,1,0:T(2,128)} reshape(f32[256,6144]{1,0:T(8,128)} %gather_fusion) | data formatting | bytes 12582912 | tf_op jit(solution)/shard_map/gather | solution.py:66
  555.0 20.2 %fusion = f32[2,128,2048]{2,1,0:T(8,128)} fusion(bf16[6144,2,2048]{2,0,1:T(8,128)(2,1)} %bitcast_dynamic-update-slice_fusion.12, pred[2]{0:T(512)(128)(4,1)S(1)} %maximum_compare_fusion, bf16[2,128,6144]{2,1,0:T(8,128)(2,1)S(1)} %bitcast.148, pred[2,128]{1,0:T(4,128)(4,1)S(1)} %copy-done.22), kind=kOutput, calls=%fused_computation.32 | convolution fusion | flops 6469189632 | bytes 55574784 | tf_op jit(solution)/shard_map/brd,dbi->bri/dot_general | solution.py:63
  575.2 3.1 fusion.10
  581.0 11.9 %multiply_reduce_fusion = bf16[128,6144]{1,0:T(8,128)(2,1)} fusion(f32[128,2,6144]{2,1,0:T(2,128)} %reshape.505, f32[128,2]{1,0:T(8,128)S(1)} %copy.20), kind=kLoop, calls=%fused_computation.35 | loop fusion | flops 2359296 | bytes 7865344 | tf_op jit(solution)/shard_map/reduce_sum | solution.py:66
  592.9 12.6 %copy.30 = bf16[768,2,2048]{2,1,0:T(2,128)(2,1)} copy(bf16[768,2,2048]{2,0,1:T(8,128)(2,1)} %reduce-scatter.5.cloned.1.call-done) | data formatting | bytes 12582912
  605.5 12.9 %psum.7 = f32[128,2]{0,1:T(2,128)} all-reduce(f32[128,2]{0,1:T(2,128)S(1)} %get-tuple-element.225), channel_id=1, replica_groups=mesh['fsdp'=8,'ep'=4] {'ep'}, use_global_device_ids=true, to_apply=%region_14.15 | all-reduce | flops 256 | bytes 2048 | tf_op jit(solution)/shard_map/psum | solution.py:82
  618.5 10.2 %reduce-scatter.3.cloned.1.call-done = bf16[128,1536]{1,0:T(8,128)(2,1)} async-done(((bf16[128,6144]{1,0:T(8,128)(2,1)}), bf16[128,1536]{1,0:T(8,128)(2,1)}) %reduce-scatter.3.cloned.1.call-update) | async-done | bytes 393232 | tf_op jit(solution)/shard_map/reduce_scatter | solution.py:77
  (130 shorter events, 65.9 us)
Async XLA Ops:
  7.2 42.2 %all-gather.5.cloned.1.call-start = ((), (), s32[]{:S(2)}) async-start(), calls=%async_computation.4 | async-start | bytes 1966080 | tf_op jit(solution)/shard_map/all_gather | solution.py:46
  7.9 274.8 %all-gather.3.cloned.1.call-start = ((), (), s32[]{:S(2)}) async-start(), calls=%async_computation.2 | async-start | bytes 56623104 | tf_op jit(solution)/shard_map/all_gather | solution.py:57
  16.3 0.7 copy-start.21
  16.3 4.7 copy-start.19
  16.4 576.5 %reduce-scatter.5.cloned.1.call-start = ((), (), s32[]{:S(2)}) async-start(), calls=%async_computation.5 | async-start | bytes 56623104 | tf_op jit(solution)/shard_map/reduce_scatter | solution.py:69
  17.1 6.4 %copy-start.17 = (s32[128,2]{0,1:T(2,128)}, s32[128,2]{0,1:T(2,128)S(1)}, u32[]{:S(2)}) copy-start(s32[128,2]{0,1:T(2,128)S(1)} %get-tuple-element.112) | copy-start | bytes 3076
  23.2 33.3 %copy-start.15 = (f32[256]{0:T(256)}, f32[256]{0:T(256)S(1)}, u32[]{:S(2)}) copy-start(f32[256]{0:T(256)S(1)} %scatter_custom_fusion) | copy-start | bytes 3076
  56.5 25.0 %copy-start.11 = (bf16[256,6144]{1,0:T(8,128)(2,1)}, bf16[256,6144]{1,0:T(8,128)(2,1)S(1)}, u32[]{:S(2)}) copy-start(bf16[256,6144]{1,0:T(8,128)(2,1)S(1)} %gather_fusion.1) | copy-start | bytes 9437188
  81.5 547.2 %reduce-scatter.3.cloned.1.call-start = ((), (), s32[]{:S(2)}) async-start(), calls=%async_computation.3 | async-start | bytes 1966080 | tf_op jit(solution)/shard_map/reduce_scatter | solution.py:77
  464.7 5.3 copy-start.1
  470.0 3.8 copy-start.2
  473.9 3.9 copy-start.3
  477.7 3.9 copy-start.4
  481.6 3.7 copy-start.5
  485.3 3.7 copy-start.6
  489.0 3.7 copy-start.7
  492.8 3.7 copy-start.8
  496.5 3.7 copy-start.9
  500.2 4.0 copy-start.10
  504.2 3.7 copy-start
  507.9 2.2 copy-start.13
  510.1 25.9 %copy-start.14 = (s32[1024]{0:T(1024)S(1)}, s32[1024]{0:T(1024)}, u32[]{:S(2)}) copy-start(s32[1024]{0:T(1024)} %pad_clamp_fusion.1) | copy-start | bytes 12292
  546.6 8.4 %copy-start.12 = (bf16[256,6144]{1,0:T(8,128)(2,1)S(1)}, bf16[256,6144]{1,0:T(8,128)(2,1)}, u32[]{:S(2)}) copy-start(bf16[256,6144]{1,0:T(8,128)(2,1)} %copy-done.11) | copy-start | bytes 9437188
  546.6 8.4 %copy-start.22 = (pred[2,128]{1,0:T(4,128)(4,1)S(1)}, pred[2,128]{1,0:T(4,128)(4,1)}, u32[]{:S(2)}) copy-start(pred[2,128]{1,0:T(4,128)(4,1)} %fusion.30) | copy-start | bytes 772
  555.0 20.2 %copy-start.16 = (f32[256]{0:T(256)S(1)}, f32[256]{0:T(256)}, u32[]{:S(2)}) copy-start(f32[256]{0:T(256)} %copy-done.15) | copy-start | bytes 3076
  578.4 2.4 copy-start.18
  578.4 2.4 copy-start.20
Sparse Core Ops, SparseCore 0:
  9.6 39.7 all-gather.4
  51.9 230.7 all-gather.2
  286.3 285.8 reduce-scatter.4
  593.0 35.6 reduce-scatter.2
where the time goes:
time: 642 us; the launch traced here: 635 us
  local copies, waits for them, and re-layouts  283 us (44%)
  waiting for transfers between devices  236 us (37%)
  matrix products  71.1 us (11%)
  other arithmetic  17 us (3%)
  between operations  14.3 us (2%)
  blocking collectives  12.9 us (2%)
    all_gather x1, waiting for transfers between devices, local(): piece = lax.all_gather(w_down, 'fsdp', axis=0, tiled=True)  200 us
    gather x48, local copies, waits for them, and re-layouts  109 us
    unnamed x73, local copies, waits for them, and re-layouts  98.7 us
    gather x1, local copies, waits for them, and re-layouts, local(): chosen = jnp.take(piece, safe_exp, axis=1)  41.5 us
    dot_general x1, matrix products, local(): jnp.einsum('bri,dbi->brd', hid_blocks, chosen, preferred_element_type=jnp...  25.9 us
    all_gather x1, waiting for transfers between devices, local(): full_grads = lax.all_gather(grad_out, 'ep', axis=1, tiled=True)  25.9 us
    dot_general x1, matrix products, local(): jnp.einsum('rd,rei->dei', scaled, masked_hid, preferred_element_type=jnp....  24.9 us
    dot_general x1, matrix products, local(): jnp.einsum('brd,dbi->bri', routed_blocks, chosen, preferred_element_type=...  20.2 us
  transfers between devices with their start and end apart: 4, of which 3 were waited for; matrix products, arithmetic and copies ran while one was open for 56% of the time, Pallas kernels for 0%

commit v1 on v0

--- a/solution.py
+++ b/solution.py
@@ -43,7 +43,14 @@
     )
     safe_exp = jnp.maximum(block_exp, 0)
     prob_valid = probs * valid.astype(jnp.float32)
-    full_grads = lax.all_gather(grad_out, "ep", axis=1, tiled=True)
+    size = lax.axis_size("ep")
+    route = [(i, (i + 1) % size) for i in range(size)]
+    parts = [grad_out]
+    for far in range(1, size):
+        parts = [lax.ppermute(parts[0], "ep", route), *parts]
+    whole = jnp.concatenate(parts, axis=1)
+    offset = (lax.axis_index("ep") + 1) * parts[-1].shape[1]
+    full_grads = jnp.roll(whole, offset, axis=1)
     model_width = full_grads.shape[1]
     routed = jnp.where(row_live[:, None] > 0, full_grads[row_tok], jnp.zeros((), jnp.bfloat16))
     scaled = (row_prob[:, None] * routed.astype(jnp.float32)).astype(jnp.bfloat16)

time: 642 us -> 612 us (0.953)
  waiting for transfers between devices: 236 us -> 206 us
    all_gather x1, waiting for transfers between devices: 200 us -> 167 us  [local(): piece = lax.all_gather(w_down, 'fsdp', axis=0, tiled=True)]
    ppermute x0 -> x3, waiting for transfers between devices: none -> 28.4 us  [local(): parts = [lax.ppermute(parts[0], 'ep', route), *parts]]
    all_gather x1 -> x0, waiting for transfers between devices: 25.9 us -> none  [local(): full_grads = lax.all_gather(grad_out, 'ep', axis=1, tiled=True)]
    unnamed x73 -> x80, local copies, waits for them, and re-layouts: 98.7 us -> 101 us
  transfers between devices with their start and end apart: 4 -> 6, of which waited for: 3 -> 5; matrix products, arithmetic and copies ran while one was open for 56% -> 57% of each run, Pallas kernels for 0% -> 0%
where the time goes in v1:
time: 612 us; the launch traced here: 605 us
  local copies, waits for them, and re-layouts  282 us (46%)
  waiting for transfers between devices  206 us (34%)
  matrix products  69.4 us (11%)
  other arithmetic  16.5 us (3%)
  between operations  14.4 us (2%)
  blocking collectives  12.8 us (2%)
    all_gather x1, waiting for transfers between devices, local(): piece = lax.all_gather(w_down, 'fsdp', axis=0, tiled=True)  167 us
    gather x48, local copies, waits for them, and re-layouts  109 us
    unnamed x80, local copies, waits for them, and re-layouts  101 us
    gather x1, local copies, waits for them, and re-layouts, local(): chosen = jnp.take(piece, safe_exp, axis=1)  41.5 us
    ppermute x3, waiting for transfers between devices, local(): parts = [lax.ppermute(parts[0], 'ep', route), *parts]  28.4 us
    dot_general x1, matrix products, local(): jnp.einsum('bri,dbi->brd', hid_blocks, chosen, preferred_element_type=jnp...  25.5 us
    dot_general x1, matrix products, local(): jnp.einsum('rd,rei->dei', scaled, masked_hid, preferred_element_type=jnp....  22.6 us
    dot_general x1, matrix products, local(): jnp.einsum('brd,dbi->bri', routed_blocks, chosen, preferred_element_type=...  21.3 us
  transfers between devices with their start and end apart: 6, of which 5 were waited for; matrix products, arithmetic and copies ran while one was open for 57% of the time, Pallas kernels for 0%

profile of v1, /device:TPU:0, one launch (start us, length us, event | category | flops | bytes accessed | tf_op | source)
XLA Modules:
  0.0 605.2 jit_solution(6639048210511241270)
XLA Ops:
  7.2 8.4 %copy.21 = bf16[768,2,2048]{2,0,1:T(8,128)(2,1)} copy(bf16[768,2,2048]{2,1,0:T(2,128)(2,1)} %param.6) | data formatting | bytes 12582912 | tf_op args[1]
  16.6 3.0 collective-permute-start
  25.5 5.2 collective-permute-done
  30.8 12.0 %collective-permute-done.1 = bf16[128,1536]{1,0:T(8,128)(2,1)S(1)} collective-permute-done((bf16[128,1536]{1,0:T(8,128)(2,1)S(1)}, bf16[128,1536]{1,0:T(8,128)(2,1)S(1)}, u32[]{:S(2)}, u32[]{:S(2)}) %collective-permute-start.1) | collective-permute-done | bytes 393248 | tf_op jit(solution)/shard_map/ppermute | solution.py:50
  43.4 11.1 %collective-permute-done.2 = bf16[128,1536]{1,0:T(8,128)(2,1)S(1)} collective-permute-done((bf16[128,1536]{1,0:T(8,128)(2,1)S(1)}, bf16[128,1536]{1,0:T(8,128)(2,1)S(1)}, u32[]{:S(2)}, u32[]{:S(2)}) %collective-permute-start.2) | collective-permute-done | bytes 393248 | tf_op jit(solution)/shard_map/ppermute | solution.py:50
  55.4 4.2 gather_fusion.1
  59.6 22.6 %convolution_convert_fusion = bf16[6144,2,2048]{2,0,1:T(8,128)(2,1)} fusion(bf16[256,6144]{1,0:T(8,128)(2,1)} %gather_fusion.1, f32[256]{0:T(256)S(1)} %scatter_custom_fusion, pred[256]{0:T(512)(128)(4,1)S(1)} %broadcast_compare_fusion, bf16[256,2]{0,1:T(2,128)(2,1)S(1)} %compare_convert_fusion, bf16[256,2048]{1,0:T(8,128)(2,1)S(1)} %copy-done.12), kind=kOutput, calls=%fused_computation.31 | convolution fusion | flops 12920553472 | bytes 54528256 | tf_op jit(solution)/shard_map/rd,rei->dei/dot_general | solution.py:77
  83.3 167.0 %all-gather.2.cloned.1.call-done = bf16[6144,2,2048]{2,0,1:T(8,128)(2,1)} async-done(((bf16[768,2,2048]{2,0,1:T(8,128)(2,1)}), bf16[6144,2,2048]{2,0,1:T(8,128)(2,1)}) %all-gather.2.cloned.1.call-update) | async-done | bytes 50331664 | tf_op jit(solution)/shard_map/all_gather | solution.py:64
  250.3 41.5 %fusion.28 = (bf16[512,2,2048]{2,0,1:T(8,128)(2,1)}, bf16[512,2,2048]{2,0,1:T(8,128)(2,1)}, bf16[512,2,2048]{2,0,1:T(8,128)(2,1)}, bf16[512,2,2048]{2,0,1:T(8,12...) fusion(bf16[6144,2,2048]{2,0,1:T(8,128)(2,1)} %all-gather.2.clo, ...), kind=kLoop, calls=%fused_computation.117 | loop fusion | bytes 100663296 | tf_op jit(solution)/shard_map/jit(_take)/gather | solution.py:66
  291.9 3.1 broadcast.318.clone
  294.9 9.6 %while.12 = (s32[]{:T(128)}, bf16[512,2,2048]{2,0,1:T(8,128)(2,1)}, s32[2,1]{0,1:T(1,128)S(1)}, bf16[2,512,2048]{2,1,0:T(8,128)(2,1)}, s32[]{:T(128)}) while((s32[]{:T(128)}, bf16[512,2,2048]{2,0,1:T(8,128)(2,1)}, s32[2,1]{0,1:T(1,128)S(1)}, bf16[2,512,2048]{2,1,0:T(8,128)(2,1)}, s32[]{:T(128)}) %tuple.161), condition=%wide.while_cond, body=%wide.while_body.sunk | while | flops 2 | bytes 4195401 | solution.py:66
  295.5 4.2 bitcast_dynamic-update-slice_fusion.36
  300.2 4.3 bitcast_dynamic-update-slice_fusion.36
  304.5 3.1 broadcast.318.clone.1
  307.6 9.4 %while.13 = (s32[]{:T(128)}, bf16[512,2,2048]{2,0,1:T(8,128)(2,1)}, s32[2,1]{0,1:T(1,128)S(1)}, bf16[2,512,2048]{2,1,0:T(8,128)(2,1)}, s32[]{:T(128)}) while((s32[]{:T(128)}, bf16[512,2,2048]{2,0,1:T(8,128)(2,1)}, s32[2,1]{0,1:T(1,128)S(1)}, bf16[2,512,2048]{2,1,0:T(8,128)(2,1)}, s32[]{:T(128)}) %tuple.203), condition=%wide.while_cond.1, body=%wide.while_body.1.sunk | while | flops 2 | bytes 4195401 | solution.py:66
  308.2 4.3 bitcast_dynamic-update-slice_fusion.37
  313.1 4.0 bitcast_dynamic-update-slice_fusion.37
  317.0 2.6 broadcast.318.clone.2
  319.6 8.8 %while.14 = (s32[]{:T(128)}, bf16[512,2,2048]{2,0,1:T(8,128)(2,1)}, s32[2,1]{0,1:T(1,128)S(1)}, bf16[2,512,2048]{2,1,0:T(8,128)(2,1)}, s32[]{:T(128)}) while((s32[]{:T(128)}, bf16[512,2,2048]{2,0,1:T(8,128)(2,1)}, s32[2,1]{0,1:T(1,128)S(1)}, bf16[2,512,2048]{2,1,0:T(8,128)(2,1)}, s32[]{:T(128)}) %tuple.204), condition=%wide.while_cond.2, body=%wide.while_body.2.sunk | while | flops 2 | bytes 4195401 | solution.py:66
  320.2 3.8 bitcast_dynamic-update-slice_fusion.38
  324.6 3.9 bitcast_dynamic-update-slice_fusion.38
  328.5 2.6 broadcast.318.clone.3
  331.0 9.2 %while.15 = (s32[]{:T(128)}, bf16[512,2,2048]{2,0,1:T(8,128)(2,1)}, s32[2,1]{0,1:T(1,128)S(1)}, bf16[2,512,2048]{2,1,0:T(8,128)(2,1)}, s32[]{:T(128)}) while((s32[]{:T(128)}, bf16[512,2,2048]{2,0,1:T(8,128)(2,1)}, s32[2,1]{0,1:T(1,128)S(1)}, bf16[2,512,2048]{2,1,0:T(8,128)(2,1)}, s32[]{:T(128)}) %tuple.205), condition=%wide.while_cond.3, body=%wide.while_body.3.sunk | while | flops 2 | bytes 4195401 | solution.py:66
  331.6 4.1 bitcast_dynamic-update-slice_fusion.39
  336.2 3.9 bitcast_dynamic-update-slice_fusion.39
  340.2 2.6 broadcast.318.clone.4
  342.8 9.1 %while.16 = (s32[]{:T(128)}, bf16[512,2,2048]{2,0,1:T(8,128)(2,1)}, s32[2,1]{0,1:T(1,128)S(1)}, bf16[2,512,2048]{2,1,0:T(8,128)(2,1)}, s32[]{:T(128)}) while((s32[]{:T(128)}, bf16[512,2,2048]{2,0,1:T(8,128)(2,1)}, s32[2,1]{0,1:T(1,128)S(1)}, bf16[2,512,2048]{2,1,0:T(8,128)(2,1)}, s32[]{:T(128)}) %tuple.206), condition=%wide.while_cond.4, body=%wide.while_body.4.sunk | while | flops 2 | bytes 4195401 | solution.py:66
  343.3 3.9 bitcast_dynamic-update-slice_fusion.40
  347.8 4.1 bitcast_dynamic-update-slice_fusion.40
  354.3 8.8 %while.17 = (s32[]{:T(128)}, bf16[512,2,2048]{2,0,1:T(8,128)(2,1)}, s32[2,1]{0,1:T(1,128)S(1)}, bf16[2,512,2048]{2,1,0:T(8,128)(2,1)}, s32[]{:T(128)}) while((s32[]{:T(128)}, bf16[512,2,2048]{2,0,1:T(8,128)(2,1)}, s32[2,1]{0,1:T(1,128)S(1)}, bf16[2,512,2048]{2,1,0:T(8,128)(2,1)}, s32[]{:T(128)}) %tuple.207), condition=%wide.while_cond.5, body=%wide.while_body.5.sunk | while | flops 2 | bytes 4195401 | solution.py:66
  354.9 3.8 bitcast_dynamic-update-slice_fusion.41
  359.3 3.8 bitcast_dynamic-update-slice_fusion.41
  363.1 2.6 broadcast.318.clone.6
  365.7 8.8 %while.18 = (s32[]{:T(128)}, bf16[512,2,2048]{2,0,1:T(8,128)(2,1)}, s32[2,1]{0,1:T(1,128)S(1)}, bf16[2,512,2048]{2,1,0:T(8,128)(2,1)}, s32[]{:T(128)}) while((s32[]{:T(128)}, bf16[512,2,2048]{2,0,1:T(8,128)(2,1)}, s32[2,1]{0,1:T(1,128)S(1)}, bf16[2,512,2048]{2,1,0:T(8,128)(2,1)}, s32[]{:T(128)}) %tuple.208), condition=%wide.while_cond.6, body=%wide.while_body.6.sunk | while | flops 2 | bytes 4195401 | solution.py:66
  366.3 3.8 bitcast_dynamic-update-slice_fusion.42
  370.7 3.9 bitcast_dynamic-update-slice_fusion.42
  377.1 9.3 %while.19 = (s32[]{:T(128)}, bf16[512,2,2048]{2,0,1:T(8,128)(2,1)}, s32[2,1]{0,1:T(1,128)S(1)}, bf16[2,512,2048]{2,1,0:T(8,128)(2,1)}, s32[]{:T(128)}) while((s32[]{:T(128)}, bf16[512,2,2048]{2,0,1:T(8,128)(2,1)}, s32[2,1]{0,1:T(1,128)S(1)}, bf16[2,512,2048]{2,1,0:T(8,128)(2,1)}, s32[]{:T(128)}) %tuple.209), condition=%wide.while_cond.7, body=%wide.while_body.7.sunk | while | flops 2 | bytes 4195401 | solution.py:66
  377.7 4.2 bitcast_dynamic-update-slice_fusion.43
  382.4 4.0 bitcast_dynamic-update-slice_fusion.43
  388.9 8.8 %while.20 = (s32[]{:T(128)}, bf16[512,2,2048]{2,0,1:T(8,128)(2,1)}, s32[2,1]{0,1:T(1,128)S(1)}, bf16[2,512,2048]{2,1,0:T(8,128)(2,1)}, s32[]{:T(128)}) while((s32[]{:T(128)}, bf16[512,2,2048]{2,0,1:T(8,128)(2,1)}, s32[2,1]{0,1:T(1,128)S(1)}, bf16[2,512,2048]{2,1,0:T(8,128)(2,1)}, s32[]{:T(128)}) %tuple.210), condition=%wide.while_cond.8, body=%wide.while_body.8.sunk | while | flops 2 | bytes 4195401 | solution.py:66
  389.5 3.8 bitcast_dynamic-update-slice_fusion.44
  393.8 3.9 bitcast_dynamic-update-slice_fusion.44
  400.2 8.7 %while.21 = (s32[]{:T(128)}, bf16[512,2,2048]{2,0,1:T(8,128)(2,1)}, s32[2,1]{0,1:T(1,128)S(1)}, bf16[2,512,2048]{2,1,0:T(8,128)(2,1)}, s32[]{:T(128)}) while((s32[]{:T(128)}, bf16[512,2,2048]{2,0,1:T(8,128)(2,1)}, s32[2,1]{0,1:T(1,128)S(1)}, bf16[2,512,2048]{2,1,0:T(8,128)(2,1)}, s32[]{:T(128)}) %tuple.211), condition=%wide.while_cond.9, body=%wide.while_body.9.sunk | while | flops 2 | bytes 4195401 | solution.py:66
  400.8 3.8 bitcast_dynamic-update-slice_fusion.45
  405.1 3.8 bitcast_dynamic-update-slice_fusion.45
  408.9 2.6 broadcast.318.clone.10
  411.5 8.9 %while.22 = (s32[]{:T(128)}, bf16[512,2,2048]{2,0,1:T(8,128)(2,1)}, s32[2,1]{0,1:T(1,128)S(1)}, bf16[2,512,2048]{2,1,0:T(8,128)(2,1)}, s32[]{:T(128)}) while((s32[]{:T(128)}, bf16[512,2,2048]{2,0,1:T(8,128)(2,1)}, s32[2,1]{0,1:T(1,128)S(1)}, bf16[2,512,2048]{2,1,0:T(8,128)(2,1)}, s32[]{:T(128)}) %tuple.212), condition=%wide.while_cond.10, body=%wide.while_body.10.sunk | while | flops 2 | bytes 4195401 | solution.py:66
  412.1 3.9 bitcast_dynamic-update-slice_fusion.46
  416.6 3.9 bitcast_dynamic-update-slice_fusion.46
  423.0 9.4 %while.23 = (s32[]{:T(128)}, bf16[512,2,2048]{2,0,1:T(8,128)(2,1)}, s32[2,1]{0,1:T(1,128)S(1)}, bf16[2,512,2048]{2,1,0:T(8,128)(2,1)}, s32[]{:T(128)}) while((s32[]{:T(128)}, bf16[512,2,2048]{2,0,1:T(8,128)(2,1)}, s32[2,1]{0,1:T(1,128)S(1)}, bf16[2,512,2048]{2,1,0:T(8,128)(2,1)}, s32[]{:T(128)}) %tuple.213), condition=%wide.while_cond.11, body=%wide.while_body.11.sunk | while | flops 2 | bytes 4195401 | solution.py:66
  423.6 4.1 bitcast_dynamic-update-slice_fusion.47
  428.2 4.2 bitcast_dynamic-update-slice_fusion.47
  432.4 5.3 bitcast_dynamic-update-slice_fusion.23
  445.4 2.5 bitcast_dynamic-update-slice_fusion.20
  475.5 2.5 bitcast_dynamic-update-slice_fusion.12
  479.0 21.3 %fusion = f32[2,128,2048]{2,1,0:T(8,128)} fusion(bf16[6144,2,2048]{2,0,1:T(8,128)(2,1)} %bitcast_dynamic-update-slice_fusion.12, pred[2]{0:T(512)(128)(4,1)S(1)} %maximum_compare_fusion, bf16[2,128,6144]{2,1,0:T(8,128)(2,1)S(1)} %bitcast.148, pred[2,128]{1,0:T(4,128)(4,1)S(1)} %fusion.30), kind=kOutput, calls=%fused_computation.32 | convolution fusion | flops 6469189632 | bytes 55574784 | tf_op jit(solution)/shard_map/brd,dbi->bri/dot_general | solution.py:70
  500.3 3.2 fusion.10
  505.9 25.5 %fusion.1 = f32[2,6144,128]{1,2,0:T(8,128)} fusion(bf16[2,128,2048]{2,1,0:T(8,128)(2,1)S(1)} %bitcast.149, bf16[6144,2,2048]{2,0,1:T(8,128)(2,1)} %bitcast_dynamic-update-slice_fusion.12, pred[2]{0:T(512)(128)(4,1)S(1)} %maximum_compare_fusion), kind=kOutput, calls=%fused_computation.33 | convolution fusion | flops 6467616768 | bytes 57671680 | tf_op jit(solution)/shard_map/bri,dbi->brd/dot_general | solution.py:67
  531.4 10.6 %gather_fusion = f32[256,6144]{1,0:T(8,128)} fusion(f32[256,6144]{1,0:T(8,128)} %bitcast.147, s32[1024]{0:T(1024)S(1)} %copy-done.14), kind=kCustom, calls=%fused_computation | custom fusion | bytes 12583936 | tf_op jit(solution)/shard_map/gather | solution.py:73
  542.0 8.4 %reshape.505 = f32[128,2,6144]{2,1,0:T(2,128)} reshape(f32[256,6144]{1,0:T(8,128)} %gather_fusion) | data formatting | bytes 12582912 | tf_op jit(solution)/shard_map/gather | solution.py:73
  550.4 11.9 %multiply_reduce_fusion = bf16[128,6144]{1,0:T(8,128)(2,1)} fusion(f32[128,2,6144]{2,1,0:T(2,128)} %reshape.505, f32[128,2]{1,0:T(8,128)S(1)} %copy.20), kind=kLoop, calls=%fused_computation.35 | loop fusion | flops 2359296 | bytes 7865344 | tf_op jit(solution)/shard_map/reduce_sum | solution.py:73
  562.3 12.6 %copy.30 = bf16[768,2,2048]{2,1,0:T(2,128)(2,1)} copy(bf16[768,2,2048]{2,0,1:T(8,128)(2,1)} %reduce-scatter.5.cloned.1.call-done) | data formatting | bytes 12582912
  574.9 12.8 %psum.7 = f32[128,2]{0,1:T(2,128)} all-reduce(f32[128,2]{0,1:T(2,128)S(1)} %get-tuple-element.225), channel_id=1, replica_groups=mesh['fsdp'=8,'ep'=4] {'ep'}, use_global_device_ids=true, to_apply=%region_14.15 | all-reduce | flops 256 | bytes 2048 | tf_op jit(solution)/shard_map/psum | solution.py:89
  587.7 10.6 %reduce-scatter.3.cloned.1.call-done = bf16[128,1536]{1,0:T(8,128)(2,1)} async-done(((bf16[128,6144]{1,0:T(8,128)(2,1)}), bf16[128,1536]{1,0:T(8,128)(2,1)}) %reduce-scatter.3.cloned.1.call-update) | async-done | bytes 393232 | tf_op jit(solution)/shard_map/reduce_scatter | solution.py:84
  (142 shorter events, 74.3 us)
Async XLA Ops:
  7.2 243.2 %all-gather.2.cloned.1.call-start = ((), (), s32[]{:S(2)}) async-start(), calls=%async_computation.2 | async-start | bytes 56623104 | tf_op jit(solution)/shard_map/all_gather | solution.py:64
  15.6 1.0 copy-start.15
  15.6 4.0 copy-start.22
  15.6 8.0 %copy-start.20 = (f32[128,2]{0,1:T(2,128)S(1)}, f32[128,2]{0,1:T(2,128)}, u32[]{:S(2)}) copy-start(f32[128,2]{0,1:T(2,128)} %param.8) | copy-start | bytes 3076
  15.6 546.7 %reduce-scatter.5.cloned.1.call-start = ((), (), s32[]{:S(2)}) async-start(), calls=%async_computation.4 | async-start | bytes 56623104 | tf_op jit(solution)/shard_map/reduce_scatter | solution.py:76
  16.6 14.2 %collective-permute-start = (bf16[128,1536]{1,0:T(8,128)(2,1)S(1)}, bf16[128,1536]{1,0:T(8,128)(2,1)S(1)}, u32[]{:S(2)}, u32[]{:S(2)}) collective-permute-start(bf16[128,1536]{1,0:T(8,128)(2,1)S(1)} %copy-done.15), channel_id=1, source_target_pairs={{0,1},{1,2},{2,3},{3,0},{4,5},{5,6},{6,7},{7,4},{8,9},{9,10},{10,1... | collective-permute-start | bytes 1179656 | tf_op jit(solution)/shard_map/ppermute | solution.py:50
  19.7 35.1 %copy-start.18 = (s32[128,2]{0,1:T(2,128)}, s32[128,2]{0,1:T(2,128)S(1)}, u32[]{:S(2)}) copy-start(s32[128,2]{0,1:T(2,128)S(1)} %get-tuple-element.112) | copy-start | bytes 3076
  25.3 34.3 %copy-start.16 = (f32[256]{0:T(256)}, f32[256]{0:T(256)S(1)}, u32[]{:S(2)}) copy-start(f32[256]{0:T(256)S(1)} %scatter_custom_fusion) | copy-start | bytes 3076
  30.8 12.1 %collective-permute-start.1 = (bf16[128,1536]{1,0:T(8,128)(2,1)S(1)}, bf16[128,1536]{1,0:T(8,128)(2,1)S(1)}, u32[]{:S(2)}, u32[]{:S(2)}) collective-permute-start(bf16[128,1536]{1,0:T(8,128)(2,1)S(1)} %collective-permute-done), channel_id=1, source_target_pairs={{0,1},{1,2},{2,3},{3,0},{4,5},{5,6},{6,7},{7,4},{8,9},{9,10},{10,1... | collective-permute-start | bytes 1179656 | tf_op jit(solution)/shard_map/ppermute | solution.py:50
  42.9 11.7 %collective-permute-start.2 = (bf16[128,1536]{1,0:T(8,128)(2,1)S(1)}, bf16[128,1536]{1,0:T(8,128)(2,1)S(1)}, u32[]{:S(2)}, u32[]{:S(2)}) collective-permute-start(bf16[128,1536]{1,0:T(8,128)(2,1)S(1)} %collective-permute-done.1), channel_id=1, source_target_pairs={{0,1},{1,2},{2,3},{3,0},{4,5},{5,6},{6,7},{7,4},{8,9},{9,10},{10,1... | collective-permute-start | bytes 1179656 | tf_op jit(solution)/shard_map/ppermute | solution.py:50
  55.4 4.2 copy-start.12
  82.2 516.2 %reduce-scatter.3.cloned.1.call-start = ((), (), s32[]{:S(2)}) async-start(), calls=%async_computation.3 | async-start | bytes 1966080 | tf_op jit(solution)/shard_map/reduce_scatter | solution.py:84
  432.4 5.3 copy-start.1
  437.6 3.8 copy-start.2
  441.5 3.9 copy-start.3
  445.4 3.8 copy-start.4
  449.2 3.7 copy-start.5
  452.9 3.7 copy-start.6
  456.7 3.7 copy-start.7
  460.4 3.8 copy-start.8
  464.1 3.7 copy-start.9
  467.8 4.0 copy-start.10
  471.8 3.7 copy-start
  475.5 3.5 copy-start.11
  479.0 21.3 %copy-start.17 = (f32[256]{0:T(256)S(1)}, f32[256]{0:T(256)}, u32[]{:S(2)}) copy-start(f32[256]{0:T(256)} %copy-done.16) | copy-start | bytes 3076
  500.3 3.2 copy-start.14
  503.6 2.2 copy-start.19
  503.6 2.2 copy-start.21
  503.6 2.3 copy-start.13
Sparse Core Ops, SparseCore 0:
  15.7 234.5 all-gather.1
  254.0 285.8 reduce-scatter.4
  562.4 35.9 reduce-scatter.2
